TPU v7x, 32 devices: a whole 2x2x4 slice. The times are simulated.
32 devices in a mesh: tm: 4 (over x, core), span: 8 (over z, y).
Axes of the slice: x: 2, y: 2, z: 4, core: 2. Of those that a mesh axis runs over, the one named last changes fastest.
Arguments:
- forcing: bfloat16 [128, 8, 16, 128], P('tm', 'span'), may hold values from -1.5 to 1.5
- iterate: bfloat16 [128, 8, 16, 128], P('tm', 'span'), may hold values from -1.5 to 1.5
- initial: bfloat16 [8, 16, 128], P('span'), may hold values from -1.5 to 1.5
- stiffness: bfloat16 [8, 128, 128], P('span'), may hold values from -0.5 to 0.5
- coupling: bfloat16 [8, 128, 128], P('span'), may hold values from -0.5 to 0.5
- pivots: bfloat16 [128, 8, 2, 128, 128], P('tm', 'span'), may hold values from -0.375 to 0.375
Outputs:
- updated: float32 [128, 8, 16, 128], P('tm', 'span')
All inputs are finite; a program needn't handle non-finite values.
Results may differ from a plain program's by a relative error of at most 0.0003.
Values may be sent and summed in bfloat16 or wider, within the bound.
A program may use at most 320 MiB of HBM per device.

v0:
```python
import math

import jax
import jax.numpy as jnp
from jax import lax
from jax.sharding import PartitionSpec as P

PRECISE = lax.Precision.HIGHEST


def passed_along(shard, axis, by):
    peers = lax.axis_size(axis)
    pairs = [(i, i + by) for i in range(peers) if 0 <= i + by < peers]
    return lax.ppermute(shard, axis, pairs)


def entering_2(shard, axis, combine, identity, reverse):
    peers, position = (lax.axis_size(axis), lax.axis_index(axis))
    everything = jax.tree.map(lambda part: lax.all_gather(part, axis), shard)
    start = jax.tree.map(
        lambda part, zero: jnp.broadcast_to(jnp.asarray(zero, part.dtype), part.shape),
        shard,
        identity,
    )

    def hop(k, before):
        at = peers - 1 - k if reverse else k
        reached = at > position if reverse else at < position
        new = combine(before, jax.tree.map(lambda part: part[at], everything))
        return jax.tree.map(lambda a, b: jnp.where(reached, a, b), new, before)

    return lax.fori_loop(0, peers, hop, start)


def phase_table(row_ids, col_ids, total):
    turned = row_ids[:, None] * col_ids[None, :] % total
    angle = turned.astype(jnp.float32) * (2.0 * math.pi / total)
    return (jnp.cos(angle), jnp.sin(angle))


def complex_product(left_real, left_imag, right_real, right_imag):
    form = "kcd,kde->kce"
    real_part = jnp.einsum(form, left_real, right_real, precision=PRECISE) - jnp.einsum(
        form, left_imag, right_imag, precision=PRECISE
    )
    imag_part = jnp.einsum(form, left_real, right_imag, precision=PRECISE) + jnp.einsum(
        form, left_imag, right_real, precision=PRECISE
    )
    return (real_part, imag_part)


def sweep_forward(spec_real, spec_imag, pivots, bonds, carry_real, carry_imag):
    count = spec_real.shape[1]

    def sweep_advance(plane_at, state):
        out_real, out_imag, into_real, into_imag = state
        pivot_now = lax.dynamic_index_in_dim(pivots, plane_at, 1, keepdims=False).astype(
            jnp.float32
        )
        bond = lax.dynamic_index_in_dim(bonds, plane_at, 0, keepdims=False)
        given_real = lax.dynamic_index_in_dim(spec_real, plane_at, 1, keepdims=False) - into_real
        given_imag = lax.dynamic_index_in_dim(spec_imag, plane_at, 1, keepdims=False) - into_imag
        pivot_real, pivot_imag = complex_product(
            given_real, given_imag, pivot_now[:, 0], pivot_now[:, 1]
        )
        next_real = jnp.einsum("kcd,de->kce", pivot_real, bond, precision=PRECISE)
        next_imag = jnp.einsum("kcd,de->kce", pivot_imag, bond, precision=PRECISE)
        out_real = lax.dynamic_update_index_in_dim(out_real, pivot_real, plane_at, 1)
        out_imag = lax.dynamic_update_index_in_dim(out_imag, pivot_imag, plane_at, 1)
        return (out_real, out_imag, next_real, next_imag)

    start = (jnp.zeros_like(spec_real), jnp.zeros_like(spec_imag), carry_real, carry_imag)
    return lax.fori_loop(0, count, sweep_advance, start)


def sweep_backward(piv_real, piv_imag, pivots, bonds, carry_real, carry_imag):
    count = piv_real.shape[1]

    def sweep_retreat(step_at, state):
        out_real, out_imag, above_real, above_imag = state
        plane_at = count - 1 - step_at
        pivot_now = lax.dynamic_index_in_dim(pivots, plane_at, 1, keepdims=False).astype(
            jnp.float32
        )
        bond = lax.dynamic_index_in_dim(bonds, plane_at, 0, keepdims=False)
        bond_real = jnp.einsum("kce,de->kcd", above_real, bond, precision=PRECISE)
        bond_imag = jnp.einsum("kce,de->kcd", above_imag, bond, precision=PRECISE)
        mixed_real, mixed_imag = complex_product(
            bond_real, bond_imag, pivot_now[:, 0], pivot_now[:, 1]
        )
        solved_real = lax.dynamic_index_in_dim(piv_real, plane_at, 1, keepdims=False) - mixed_real
        solved_imag = lax.dynamic_index_in_dim(piv_imag, plane_at, 1, keepdims=False) - mixed_imag
        out_real = lax.dynamic_update_index_in_dim(out_real, solved_real, plane_at, 1)
        out_imag = lax.dynamic_update_index_in_dim(out_imag, solved_imag, plane_at, 1)
        return (out_real, out_imag, solved_real, solved_imag)

    start = (jnp.zeros_like(piv_real), jnp.zeros_like(piv_imag), carry_real, carry_imag)
    return lax.fori_loop(0, count, sweep_retreat, start)


def forward_map(pivots, bonds, identity_map):
    count = bonds.shape[0]

    def forward_advance(plane_at, state):
        map_real, map_imag = state
        pivot_now = lax.dynamic_index_in_dim(pivots, plane_at, 1, keepdims=False).astype(
            jnp.float32
        )
        bond = lax.dynamic_index_in_dim(bonds, plane_at, 0, keepdims=False)
        mixed_real, mixed_imag = complex_product(
            map_real, map_imag, pivot_now[:, 0], pivot_now[:, 1]
        )
        next_real = jnp.einsum("kcd,de->kce", mixed_real, bond, precision=PRECISE)
        next_imag = jnp.einsum("kcd,de->kce", mixed_imag, bond, precision=PRECISE)
        return (-next_real, -next_imag)

    return lax.fori_loop(0, count, forward_advance, (identity_map, jnp.zeros_like(identity_map)))


def backward_map(pivots, bonds, identity_map):
    count = bonds.shape[0]

    def backward_retreat(step_at, state):
        map_real, map_imag = state
        plane_at = count - 1 - step_at
        pivot_now = lax.dynamic_index_in_dim(pivots, plane_at, 1, keepdims=False).astype(
            jnp.float32
        )
        bond = lax.dynamic_index_in_dim(bonds, plane_at, 0, keepdims=False)
        bond_real = jnp.einsum("kce,de->kcd", map_real, bond, precision=PRECISE)
        bond_imag = jnp.einsum("kce,de->kcd", map_imag, bond, precision=PRECISE)
        next_real, next_imag = complex_product(
            bond_real, bond_imag, pivot_now[:, 0], pivot_now[:, 1]
        )
        return (-next_real, -next_imag)

    return lax.fori_loop(0, count, backward_retreat, (identity_map, jnp.zeros_like(identity_map)))


def compose(earlier, later):
    first_real, first_imag, first_vreal, first_vimag = earlier
    second_real, second_imag, second_vreal, second_vimag = later
    map_real, map_imag = complex_product(first_real, first_imag, second_real, second_imag)
    vec_real, vec_imag = complex_product(first_vreal, first_vimag, second_real, second_imag)
    return (map_real, map_imag, vec_real + second_vreal, vec_imag + second_vimag)


def on_device(forcing, iterate, initial, stiffness, coupling, pivots):
    steps_here = forcing.shape[0]
    dof_count = forcing.shape[3]
    total_steps = steps_here * lax.axis_size("tm")
    tm_pos = lax.axis_index("tm")
    last_step = passed_along(iterate[steps_here - 1], "tm", 1)
    first_prior = jnp.where(tm_pos == 0, initial, last_step)
    prior_state = jnp.concatenate([first_prior[None], iterate[:-1]], 0)
    own_term = jnp.einsum("njcd,jde->njce", iterate, stiffness, preferred_element_type=jnp.float32)
    lower_edge = jnp.einsum(
        "ncd,de->nce", iterate[:, -1], coupling[-1], preferred_element_type=jnp.float32
    )
    from_below = passed_along(lower_edge, "span", 1)
    upper_plane = passed_along(iterate[:, 0], "span", -1)
    below_local = jnp.einsum(
        "njcd,jde->njce", iterate[:, :-1], coupling[:-1], preferred_element_type=jnp.float32
    )
    below = jnp.concatenate([from_below[:, None], below_local], 1)
    above_source = jnp.concatenate([iterate[:, 1:], upper_plane[:, None]], 1)
    above = jnp.einsum("njce,jde->njcd", above_source, coupling, preferred_element_type=jnp.float32)
    resid = (
        forcing.astype(jnp.float32)
        - iterate.astype(jnp.float32)
        + prior_state.astype(jnp.float32)
        - (own_term + below + above)
    )
    own_ids = tm_pos * steps_here + jnp.arange(steps_here, dtype=jnp.int32)
    gamma = jnp.float32(0.5) ** (own_ids.astype(jnp.float32) / total_steps)
    scaled = resid * gamma[:, None, None, None]
    row_ids = jnp.arange(lax.axis_size("tm") * steps_here, dtype=jnp.int32)
    cosine, sine_table = phase_table(row_ids, own_ids, total_steps)
    real_part = jnp.tensordot(cosine, scaled, axes=1, precision=PRECISE)
    imag_part = -jnp.tensordot(sine_table, scaled, axes=1, precision=PRECISE)
    spectrum = lax.psum_scatter(
        jnp.stack([real_part, imag_part], 1), "tm", scatter_dimension=0, tiled=True
    )
    spec_real = spectrum[:, 0]
    spec_imag = spectrum[:, 1]
    bonds = coupling.astype(jnp.float32)
    identity_map = jnp.broadcast_to(
        jnp.eye(dof_count, dtype=jnp.float32), (steps_here, dof_count, dof_count)
    )
    zero_vec = jnp.zeros_like(spec_real[:, 0])
    start_maps = (identity_map, jnp.zeros_like(identity_map), zero_vec, zero_vec)
    fwd_real, fwd_imag = forward_map(pivots, bonds, identity_map)
    trial = sweep_forward(spec_real, spec_imag, pivots, bonds, zero_vec, zero_vec)
    entering = entering_2(
        (fwd_real, fwd_imag, trial[2], trial[3]), "span", compose, start_maps, False
    )
    swept = sweep_forward(spec_real, spec_imag, pivots, bonds, entering[2], entering[3])
    back_real, back_imag = backward_map(pivots, bonds, identity_map)
    trial_back = sweep_backward(swept[0], swept[1], pivots, bonds, zero_vec, zero_vec)
    from_above = entering_2(
        (back_real, back_imag, trial_back[2], trial_back[3]), "span", compose, start_maps, True
    )
    solved = sweep_backward(swept[0], swept[1], pivots, bonds, from_above[2], from_above[3])
    row_ids = jnp.arange(lax.axis_size("tm") * steps_here, dtype=jnp.int32)
    cosine, sine_table = phase_table(row_ids, own_ids, total_steps)
    correction = lax.psum_scatter(
        (
            jnp.tensordot(cosine, solved[0], axes=1, precision=PRECISE)
            - jnp.tensordot(sine_table, solved[1], axes=1, precision=PRECISE)
        )
        * (1.0 / total_steps),
        "tm",
        scatter_dimension=0,
        tiled=True,
    )
    return iterate.astype(jnp.float32) + correction / gamma[:, None, None, None]


def solution(mesh):
    return jax.shard_map(
        on_device,
        mesh=mesh,
        in_specs=(
            P("tm", "span", None, None),
            P("tm", "span", None, None),
            P("span", None, None),
            P("span", None, None),
            P("span", None, None),
            P("tm", "span", None, None, None),
        ),
        out_specs=P("tm", "span", None, None),
        check_vma=False,
    )
```

profile of v0, /device:TPU:1, one launch (start us, length us, event | category | flops | bytes accessed | tf_op | source)
XLA Modules:
  0.0 1325.9 jit_solution(1516541709668842577)
XLA Ops:
  8.4 4.0 collective-permute-start.1
  13.0 3.9 collective-permute-start
  31.0 29.5 %reduce-scatter.3.cloned.1.call-done = f32[32,2,1,16,128]{4,0,3,2,1:T(8,128)} async-done(((f32[128,2,1,16,128]{4,0,3,2,1:T(8,128)}), f32[32,2,1,16,128]{4,0,3,2,1:T(8,128)}) %reduce-scatter.3.cloned.1.call-update) | async-done | bytes 524304 | tf_op jit(solution)/shard_map/reduce_scatter | solution.py:181
  92.3 19.6 %all-gather.21.cloned.1.call-done = f32[256,16,128]{2,1,0:T(8,128)} async-done(((f32[32,16,128]{2,1,0:T(8,128)}), f32[256,16,128]{2,1,0:T(8,128)}) %all-gather.21.cloned.1.call-update) | async-done | bytes 2097168 | tf_op jit(solution)/shard_map/all_gather | solution.py:19
  111.9 49.8 %all-gather.23.cloned.1.call-done = f32[256,16,128]{2,1,0:T(8,128)} async-done(((f32[32,16,128]{2,1,0:T(8,128)}), f32[256,16,128]{2,1,0:T(8,128)}) %all-gather.23.cloned.1.call-update) | async-done | bytes 2097168 | tf_op jit(solution)/shard_map/all_gather | solution.py:19
  161.7 229.0 %all-gather.17.cloned.1.call-done = f32[256,128,128]{2,1,0:T(8,128)} async-done(((f32[32,128,128]{2,1,0:T(8,128)}), f32[256,128,128]{2,1,0:T(8,128)}) %all-gather.17.cloned.1.call-update) | async-done | bytes 16777232 | tf_op jit(solution)/shard_map/all_gather | solution.py:19
  390.7 227.5 %all-gather.19.cloned.1.call-done = f32[256,128,128]{2,1,0:T(8,128)} async-done(((f32[32,128,128]{2,1,0:T(8,128)}), f32[256,128,128]{2,1,0:T(8,128)}) %all-gather.19.cloned.1.call-update) | async-done | bytes 16777232 | tf_op jit(solution)/shard_map/all_gather | solution.py:19
  618.2 113.6 %while.22 = (s32[]{:T(128)}, f32[32,16,128]{2,1,0:T(8,128)S(1)}, f32[32,16,128]{2,1,0:T(8,128)S(1)}, s32[]{:T(128)}, f32[8,32,128,128]{3,2,1,0:T(8,128)}, /*inde...) while((s32[]{:T(128)}, f32[32,16,128]{2,1,0:T(8,128)S(1)}, ...), condition=%wide.region_2.3_spmd.clone, body=%wide.region_1.2_spmd.clone.sunk | while | flops 403439616 | bytes 13112457 | solution.py:32
  625.4 3.8 fusion.276
  629.1 3.7 fusion.278
  639.8 3.5 fusion.276
  643.4 3.5 fusion.278
  653.9 3.5 fusion.276
  657.4 3.5 fusion.278
  668.0 3.5 fusion.276
  706.6 4.1 fusion.275
  710.7 3.5 fusion.276
  714.3 3.5 fusion.278
  738.6 107.0 %all-gather.25.cloned.1.call-done = f32[256,128,128]{2,1,0:T(8,128)} async-done(((f32[32,128,128]{2,1,0:T(8,128)}), f32[256,128,128]{2,1,0:T(8,128)}) %all-gather.25.cloned.1.call-update) | async-done | bytes 16777232 | tf_op jit(solution)/shard_map/all_gather | solution.py:19
  845.6 227.6 %all-gather.27.cloned.1.call-done = f32[256,128,128]{2,1,0:T(8,128)} async-done(((f32[32,128,128]{2,1,0:T(8,128)}), f32[256,128,128]{2,1,0:T(8,128)}) %all-gather.27.cloned.1.call-update) | async-done | bytes 16777232 | tf_op jit(solution)/shard_map/all_gather | solution.py:19
  1073.2 48.2 %all-gather.29.cloned.1.call-done = f32[256,16,128]{2,1,0:T(8,128)} async-done(((f32[32,16,128]{2,1,0:T(8,128)}), f32[256,16,128]{2,1,0:T(8,128)}) %all-gather.29.cloned.1.call-update) | async-done | bytes 2097168 | tf_op jit(solution)/shard_map/all_gather | solution.py:19
  1121.5 49.8 %all-gather.31.cloned.1.call-done = f32[256,16,128]{2,1,0:T(8,128)} async-done(((f32[32,16,128]{2,1,0:T(8,128)}), f32[256,16,128]{2,1,0:T(8,128)}) %all-gather.31.cloned.1.call-update) | async-done | bytes 2097168 | tf_op jit(solution)/shard_map/all_gather | solution.py:19
  1171.3 112.7 %while.23 = (s32[]{:T(128)}, f32[32,16,128]{2,1,0:T(8,128)S(1)}, f32[32,16,128]{2,1,0:T(8,128)S(1)}, s32[]{:T(128)}, f32[8,32,128,128]{3,2,1,0:T(8,128)}, /*inde...) while((s32[]{:T(128)}, f32[32,16,128]{2,1,0:T(8,128)S(1)}, ...), condition=%wide.region_4.5_spmd.clone, body=%wide.region_3.4_spmd.clone.sunk | while | flops 403439616 | bytes 13112519 | solution.py:32
  1291.6 25.2 %reduce-scatter.5.cloned.1.call-done = f32[32,1,16,128]{3,0,2,1:T(8,128)} async-done(((f32[128,1,16,128]{3,0,2,1:T(8,128)}), f32[32,1,16,128]{3,0,2,1:T(8,128)}) %reduce-scatter.5.cloned.1.call-update) | async-done | bytes 262160 | tf_op jit(solution)/shard_map/reduce_scatter | solution.py:206
  (187 shorter events, 253.2 us)
Async XLA Ops:
  6.5 0.8 copy-start
  6.5 54.0 %reduce-scatter.3.cloned.1.call-start = ((), (), s32[]{:S(2)}) async-start(), calls=%async_computation.2 | async-start | bytes 2621440 | tf_op jit(solution)/shard_map/reduce_scatter | solution.py:181
  8.4 15.6 %collective-permute-start.1 = (f32[32,16,128]{2,0,1:T(8,128)S(1)}, f32[32,16,128]{2,0,1:T(8,128)S(1)}, u32[]{:S(2)}, u32[]{:S(2)}) collective-permute-start(f32[32,16,128]{2,0,1:T(8,128)S(1)} %fusion.159), channel_id=1, source_target_pairs={{0,1},{1,2},{2,3},{3,4},{4,5},{5,6},{6,7},{8,9},{9,10},{10,11},{11... | collective-permute-start | bytes 786440 | tf_op jit(solution)/shard_map/ppermute | solution.py:14
  13.0 8.3 collective-permute-start
  17.9 6.0 collective-permute-start.2
  29.1 82.8 %all-gather.21.cloned.1.call-start = ((), (), s32[]{:S(2)}) async-start(), calls=%async_computation.6 | async-start | bytes 2359296 | tf_op jit(solution)/shard_map/all_gather | solution.py:19
  64.4 97.3 %all-gather.23.cloned.1.call-start = ((), (), s32[]{:S(2)}) async-start(), calls=%async_computation.7 | async-start | bytes 2359296 | tf_op jit(solution)/shard_map/all_gather | solution.py:19
  67.3 323.4 %all-gather.17.cloned.1.call-start = ((), (), s32[]{:S(2)}) async-start(), calls=%async_computation.4 | async-start | bytes 18874368 | tf_op jit(solution)/shard_map/all_gather | solution.py:19
  71.8 546.4 %all-gather.19.cloned.1.call-start = ((), (), s32[]{:S(2)}) async-start(), calls=%async_computation.5 | async-start | bytes 18874368 | tf_op jit(solution)/shard_map/all_gather | solution.py:19
  76.9 768.7 %all-gather.25.cloned.1.call-start = ((), (), s32[]{:S(2)}) async-start(), calls=%async_computation.8 | async-start | bytes 18874368 | tf_op jit(solution)/shard_map/all_gather | solution.py:19
  77.9 2.2 copy-start.1
  78.9 1.4 copy-start.3
  83.0 990.2 %all-gather.27.cloned.1.call-start = ((), (), s32[]{:S(2)}) async-start(), calls=%async_computation.9 | async-start | bytes 18874368 | tf_op jit(solution)/shard_map/all_gather | solution.py:19
  83.1 2.9 copy-start.2
  88.7 1032.8 %all-gather.29.cloned.1.call-start = ((), (), s32[]{:S(2)}) async-start(), calls=%async_computation.10 | async-start | bytes 2359296 | tf_op jit(solution)/shard_map/all_gather | solution.py:19
  734.0 1.9 copy-start.7
  734.0 1.9 copy-start.8
  735.9 1.9 copy-start.5
  737.8 433.4 %all-gather.31.cloned.1.call-start = ((), (), s32[]{:S(2)}) async-start(), calls=%async_computation.11 | async-start | bytes 2359296 | tf_op jit(solution)/shard_map/all_gather | solution.py:19
  738.6 578.3 %reduce-scatter.5.cloned.1.call-start = ((), (), s32[]{:S(2)}) async-start(), calls=%async_computation.3 | async-start | bytes 1310720 | tf_op jit(solution)/shard_map/reduce_scatter | solution.py:206
  1284.0 2.4 copy-start.6
  1286.1 2.4 copy-start.9
  1289.4 27.4 %copy-start.4 = (bf16[32,1,16,128]{3,2,1,0:T(8,128)(2,1)S(1)}, bf16[32,1,16,128]{3,2,1,0:T(8,128)(2,1)}, u32[]{:S(2)}) copy-start(bf16[32,1,16,128]{3,2,1,0:T(8,128)(2,1)} %param.11) | copy-start | bytes 393220
Sparse Core Ops, SparseCore 0:
  29.3 31.1 reduce-scatter.2
  64.5 47.3 all-gather.20
  114.0 47.5 all-gather.22
  163.7 227.0 all-gather.16
  392.7 225.4 all-gather.18
  620.1 225.4 all-gather.24
  847.8 225.4 all-gather.26
  1075.4 46.0 all-gather.28
  1123.6 47.5 all-gather.30
  1291.8 25.0 reduce-scatter.4
where the time goes:
time: 1340 us; the launch traced here: 1330 us
  waiting for transfers between devices  1020 us (76%)
  matrix products  272 us (20%)
  between operations  14.2 us (1%)
    all_gather x8, waiting for transfers between devices, entering_2(): everything = jax.tree.map(lambda part: lax.all_gather(part, axis), shard)  958 us
    dot_general x22, matrix products, complex_product(): jnp.einsum(form, left_imag, right_imag, precision=PRECISE)  64.5 us
    dot_general x21, matrix products, complex_product(): jnp.einsum(form, left_imag, right_real, precision=PRECISE)  63.5 us
    dot_general x22, matrix products, complex_product(): jnp.einsum(form, left_real, right_real, precision=PRECISE)  62.8 us
    dot_general x21, matrix products, complex_product(): jnp.einsum(form, left_real, right_imag, precision=PRECISE)  62.4 us
    reduce_scatter x1, waiting for transfers between devices, on_device(): lax.psum_scatter(jnp.stack([real_part, imag_part], 1), 'tm', scatter_dime...  29.5 us
  transfers between devices with their start and end apart: 13, of which 11 were waited for; matrix products, arithmetic and copies ran while one was open for 11% of the time, Pallas kernels for 0%

commit v1 on v0

v1 whole, which is shorter than its diff:
```python
import functools
import math

import jax
import jax.numpy as jnp
import numpy as np
from jax import lax
from jax.experimental import pallas as pl
from jax.experimental.pallas import tpu as pltpu
from jax.sharding import PartitionSpec as P

MESH = pl.DeviceIdType.MESH
F32 = jnp.float32
BF16 = jnp.bfloat16


def split(value):
    high = value.astype(BF16)
    low = (value - high.astype(F32)).astype(BF16)
    return high, low


def dot(a, b):
    return jnp.dot(a, b, preferred_element_type=F32)


def tables(total, blocks):
    ids = np.arange(total)
    theta = 2.0 * math.pi / total * ((ids[:, None] * ids[None, :]) % total)
    gamma = 0.5 ** (ids / total)
    here = total // blocks

    def three(table):
        high = table.astype(np.float32).astype(jnp.bfloat16)
        low = (table - high.astype(np.float64)).astype(np.float32).astype(jnp.bfloat16)
        return np.concatenate([high, high, low], -1)

    cosine = (np.cos(theta) * gamma).reshape(blocks, here, total)
    sine = (-np.sin(theta) * gamma).reshape(blocks, here, total)
    forward = three(np.concatenate([cosine, sine], 1))
    back = 1.0 / (total * gamma[:, None])
    cosine = (np.cos(theta) * back).reshape(total, blocks, here).transpose(1, 0, 2)
    sine = (-np.sin(theta) * back).reshape(total, blocks, here).transpose(1, 0, 2)
    inverse = three(np.concatenate([cosine, sine], 2))
    return forward, inverse


def kernel(
    n_tm, n_sp, chunks, cases, forcing, iterate, initial, stiff, coup, pivots, tf, ti, out,
    it_below, it_above, c_below, prior0, gath, weights, c2, ct2, spec, pv, q_in, q_out, x_in, x_out,
    contrib, rs1, rs2,
    nb_send, nb_recv, ag_send, ag_recv, f_send, f_recv, b_send, b_recv,
    r1_send, r1_recv, r2_send, r2_recv,
):
    tm, sp = lax.axis_index("tm"), lax.axis_index("span")
    rows, dof = iterate.shape
    steps = rows // cases
    total = steps * n_tm
    per = steps // chunks
    n_x = n_tm // 2
    core, x = tm % 2, tm // 2
    sib = 2 * x + 1 - core
    last = n_sp - 1
    has_below, has_above = sp > 0, sp < last

    def copy(src, dst, send, recv, **where):
        return pltpu.make_async_remote_copy(
            src_ref=src, dst_ref=dst, send_sem=send, recv_sem=recv, device_id=where, device_id_type=MESH
        )

    def block(b):
        return pl.ds(pl.multiple_of(b * rows, rows), rows)

    barrier = pltpu.get_barrier_semaphore()
    for i in range(1, n_tm):
        pl.semaphore_signal(barrier, inc=1, device_id={"tm": (tm + i) % n_tm}, device_id_type=MESH)

    @pl.when(has_below)
    def _():
        pl.semaphore_signal(barrier, inc=1, device_id={"span": sp - 1}, device_id_type=MESH)

    @pl.when(has_above)
    def _():
        pl.semaphore_signal(barrier, inc=1, device_id={"span": sp + 1}, device_id_type=MESH)

    pl.semaphore_wait(
        barrier, n_tm - 1 + has_below.astype(jnp.int32) + has_above.astype(jnp.int32)
    )

    to_up = copy(iterate, it_below, nb_send.at[0], nb_recv.at[0], span=sp + 1)
    to_down = copy(iterate, it_above, nb_send.at[1], nb_recv.at[1], span=sp - 1)
    c_up = copy(coup, c_below, nb_send.at[2], nb_recv.at[2], span=sp + 1)
    to_next = copy(
        iterate.at[pl.ds(rows - cases, cases)], prior0, nb_send.at[3], nb_recv.at[3], tm=tm + 1
    )

    @pl.when(tm < n_tm - 1)
    def _():
        to_next.start()

    @pl.when(has_above)
    def _():
        to_up.start()
        c_up.start()

    @pl.when(has_below)
    def _():
        to_down.start()

    mine = block(tm)
    it_wide = iterate[...].astype(F32)
    own = forcing[...].astype(F32) - it_wide - dot(iterate[...], stiff[...])
    own = own + jnp.concatenate([jnp.zeros((cases, dof), F32), it_wide[: rows - cases]], 0)
    gath[mine] = own
    first = pl.ds(pl.multiple_of(tm * rows, rows), cases)

    zero = jnp.zeros((dof, dof), BF16)
    bond = coup[...]
    bond_t = bond.astype(F32).T.astype(BF16)
    for ref, value in ((c2, bond), (ct2, bond_t)):
        ref[:dof, :dof] = value
        ref[dof:, dof:] = value
        ref[:dof, dof:] = zero
        ref[dof:, :dof] = zero

    def build(k, carry):
        real, imag = pivots[k, 0], pivots[k, 1]
        weights[k, :dof, :dof] = real
        weights[k, dof:, dof:] = real
        weights[k, :dof, dof:] = imag
        weights[k, dof:, :dof] = -imag
        return carry

    @pl.when(tm == 0)
    def _():
        gath[first] = gath[first] + initial[...].astype(F32)

    @pl.when(tm > 0)
    def _():
        to_next.wait_recv()
        gath[first] = gath[first] + prior0[...].astype(F32)

    @pl.when(has_above)
    def _():
        to_down.wait_recv()
        gath[mine] = gath[mine] - dot(it_above[...], ct2[:dof, :dof])

    @pl.when(has_below)
    def _():
        to_up.wait_recv()
        c_up.wait_recv()
        gath[mine] = gath[mine] - dot(it_below[...], c_below[...])

    def send_block(b, slot, peer):
        at = block(b)
        return copy(gath.at[at], gath.at[at], ag_send.at[slot], ag_recv.at[b], tm=peer)

    for i in range(1, n_x):
        send_block(tm, i, 2 * ((x + i) % n_x) + core).start()
    send_block(tm, 0, sib).start()
    lax.fori_loop(0, steps, build, 0)

    @pl.when(sp == 0)
    def _():
        q_in[...] = jnp.zeros_like(q_in)

    for i in range(1, n_x):
        b = 2 * ((x + n_x - i) % n_x) + core
        send_block(b, 0, sib).wait_recv()
        send_block(b, n_x + i, sib).start()
    for i in range(n_x):
        send_block(2 * ((x + n_x - i) % n_x) + 1 - core, 0, sib).wait_recv()

    forward = tf[tm]
    for case in range(0, cases, 2):
        value = jnp.concatenate(
            [gath[pl.ds(case + i, total, stride=cases), :] for i in range(2)], 1
        )
        high, low = split(value)
        result = dot(forward, jnp.concatenate([high, low, high], 0))
        for i in range(2):
            part = result[:, i * dof : (i + 1) * dof]
            spec[0, pl.ds(case + i, steps, stride=cases), :] = part[:steps]
            spec[1, pl.ds(case + i, steps, stride=cases), :] = part[steps:]

    size = per * cases

    def at_chunk(c):
        return pl.ds(pl.multiple_of(c * size, size), size)

    def f_copy(c):
        at = at_chunk(c)
        return copy(q_out.at[:, at], q_in.at[:, at], f_send.at[c], f_recv.at[c], span=sp + 1)

    def b_copy(c):
        at = at_chunk(c)
        return copy(x_out.at[:, at], x_in.at[:, at], b_send.at[c], b_recv.at[c], span=sp - 1)

    def wide(ref, at):
        return jnp.concatenate([ref[0, at, :], ref[1, at, :]], 1)

    def put(ref, at, value):
        ref[0, at, :] = value[:, :dof]
        ref[1, at, :] = value[:, dof:]

    def times_pivots(value, c):
        high, low = split(value)
        parts = []
        for f in range(per):
            at = slice(f * cases, (f + 1) * cases)
            both = dot(jnp.concatenate([high[at], low[at]], 0), weights[c * per + f])
            parts.append(both[:cases] + both[cases:])
        return jnp.concatenate(parts, 0)

    def times_bond(value, ref):
        both = dot(jnp.concatenate(split(value), 0), ref[...])
        return both[:size] + both[size:]

    def up(c):
        at = at_chunk(c)

        @pl.when(has_below)
        def _():
            f_copy(c).wait_recv()

        pivoted = times_pivots(wide(spec, at) - wide(q_in, at), c)

        @pl.when(has_above)
        def _():
            put(q_out, at, times_bond(pivoted, c2))
            f_copy(c).start()
            put(pv, at, pivoted)

        @pl.when(sp == last)
        def _():
            put(x_out, at, pivoted)
            b_copy(c).start()

    def down(c):
        at = at_chunk(c)
        b_copy(c).wait_recv()
        put(x_out, at, wide(pv, at) - times_pivots(times_bond(wide(x_in, at), ct2), c))

        @pl.when(has_below)
        def _():
            b_copy(c).start()

    lag = jnp.minimum(chunks, 3 * (last - sp))

    def turn(t, carry):
        @pl.when(t < chunks)
        def _():
            up(t)

        @pl.when(has_above & (t >= lag) & (t < lag + chunks))
        def _():
            down(t - lag)

        return carry

    lax.fori_loop(0, 2 * chunks, turn, 0)

    inverse = ti[tm]
    for case in range(0, cases, 2):
        value = jnp.concatenate(
            [
                jnp.concatenate(
                    [x_out[p, pl.ds(case + i, steps, stride=cases), :] for p in range(2)], 0
                )
                for i in range(2)
            ],
            1,
        )
        high, low = split(value)
        result = dot(inverse, jnp.concatenate([high, low, high], 0))
        for i in range(2):
            contrib[pl.ds(case + i, total, stride=cases), :] = result[:, i * dof : (i + 1) * dof]

    def r1_copy(i):
        there = (x + i) % n_x
        return copy(
            contrib.at[block(2 * there + 1 - core)], rs1.at[i], r1_send.at[i], r1_recv.at[i], tm=sib
        )

    def r2_copy(i):
        there = (x + i) % n_x
        return copy(
            contrib.at[block(2 * there + core)], rs2.at[i], r2_send.at[i], r2_recv.at[i],
            tm=2 * there + core,
        )

    order = list(range(1, n_x)) + [0]
    for i in order:
        r1_copy(i).start()
    for i in order:
        r1_copy(i).wait_recv()
        at = block(2 * ((x + i) % n_x) + core)
        contrib[at] = contrib[at] + rs1[i]
        if i:
            r2_copy(i).start()
    result = contrib[mine] + iterate[...].astype(F32)
    for i in range(1, n_x):
        r2_copy(i).wait_recv()
        result = result + rs2[i]
    out[...] = result

    @pl.when(tm < n_tm - 1)
    def _():
        to_next.wait_send()

    @pl.when(has_above)
    def _():
        to_up.wait_send()
        c_up.wait_send()

    @pl.when(has_below)
    def _():
        to_down.wait_send()

    for slot in range(2 * n_x):
        if slot != n_x:
            send_block(tm, slot, sib).wait_send()

    def drain(c, carry):
        @pl.when(has_above)
        def _():
            f_copy(c).wait_send()

        @pl.when(has_below)
        def _():
            b_copy(c).wait_send()

        return carry

    lax.fori_loop(0, chunks, drain, 0)
    for i in range(n_x):
        r1_copy(i).wait_send()
    for i in range(1, n_x):
        r2_copy(i).wait_send()


def on_device(n_tm, n_sp, forcing, iterate, initial, stiffness, coupling, pivots):
    steps, planes, cases, dof = forcing.shape
    assert planes == 1 and n_tm % 2 == 0 and n_sp > 1
    rows, total, n_x = steps * cases, steps * n_tm, n_tm // 2
    chunks = math.gcd(steps, 8)
    forward, inverse = tables(total, n_tm)
    state = pltpu.VMEM((2, rows, dof), F32)
    dma = pltpu.SemaphoreType.DMA
    vmem = pl.BlockSpec(memory_space=pltpu.VMEM)
    result = pl.pallas_call(
        functools.partial(kernel, n_tm, n_sp, chunks, cases),
        out_shape=jax.ShapeDtypeStruct((rows, dof), F32),
        in_specs=[vmem] * 8,
        out_specs=vmem,
        scratch_shapes=[
            pltpu.VMEM((rows, dof), BF16),
            pltpu.VMEM((rows, dof), BF16),
            pltpu.VMEM((dof, dof), BF16),
            pltpu.VMEM((cases, dof), BF16),
            pltpu.VMEM((total * cases, dof), F32),
            pltpu.VMEM((steps, 2 * dof, 2 * dof), BF16),
            pltpu.VMEM((2 * dof, 2 * dof), BF16),
            pltpu.VMEM((2 * dof, 2 * dof), BF16),
            state, state, state, state, state, state,
            pltpu.VMEM((total * cases, dof), F32),
            pltpu.VMEM((n_x, rows, dof), F32),
            pltpu.VMEM((n_x, rows, dof), F32),
            dma((4,)), dma((4,)), dma((2 * n_x,)), dma((n_tm,)),
            dma((chunks,)), dma((chunks,)), dma((chunks,)), dma((chunks,)),
            dma((n_x,)), dma((n_x,)), dma((n_x,)), dma((n_x,)),
        ],
        compiler_params=pltpu.CompilerParams(
            collective_id=0, has_side_effects=True, vmem_limit_bytes=48 * 2**20
        ),
    )(
        forcing.reshape(rows, dof),
        iterate.reshape(rows, dof),
        initial.reshape(cases, dof),
        stiffness.reshape(dof, dof),
        coupling.reshape(dof, dof),
        pivots.reshape(steps, 2, dof, dof),
        jnp.asarray(forward),
        jnp.asarray(inverse),
    )
    return result.reshape(steps, 1, cases, dof)


def solution(mesh):
    return jax.shard_map(
        functools.partial(on_device, mesh.shape["tm"], mesh.shape["span"]),
        mesh=mesh,
        in_specs=(
            P("tm", "span", None, None),
            P("tm", "span", None, None),
            P("span", None, None),
            P("span", None, None),
            P("span", None, None),
            P("tm", "span", None, None, None),
        ),
        out_specs=P("tm", "span", None, None),
        check_vma=False,
    )
```

time: 1340 us -> 107 us (0.08)
  waiting for transfers between devices: 1020 us -> 0 us
  matrix products: 272 us -> 0 us
  Pallas kernels: 0 us -> 98.1 us
  between operations: 14.2 us -> 0.02 us
    all_gather x8 -> x0, waiting for transfers between devices: 958 us -> none  [entering_2(): everything = jax.tree.map(lambda part: lax.all_gather(part, axis), shard)]
    dot_general x102 -> x0, matrix products: 272 us -> none  [the longest x22 64.5 us: complex_product(): jnp.einsum(form, left_imag, right_imag, precision=PRECISE)]
    pallas_call x0 -> x1, Pallas kernels: none -> 98.1 us  [on_device(): pl.pallas_call(functools.partial(kernel, n_tm, n_sp, chunks, cases), out_...]
    reduce_scatter x2 -> x0, waiting for transfers between devices: 54.7 us -> none  [the longest x1 29.5 us: on_device(): lax.psum_scatter(jnp.stack([real_part, imag_part], 1), 'tm', scatter_dime...]
  transfers between devices with their start and end apart: 13 -> 0, of which waited for: 11 -> 0; matrix products, arithmetic and copies ran while one was open for 11% -> 0% of each run, Pallas kernels for 0% -> 0%
where the time goes in v1:
time: 107 us; the launch traced here: 106 us
  Pallas kernels  98.1 us (92%)
  local copies, waits for them, and re-layouts  8.18 us (8%)
    pallas_call x1, Pallas kernels, on_device(): pl.pallas_call(functools.partial(kernel, n_tm, n_sp, chunks, cases), out_...  98.1 us
    unnamed x17, local copies, waits for them, and re-layouts  8.18 us

profile of v1, /device:TPU:1, one launch (start us, length us, event | category | flops | bytes accessed | tf_op | source)
XLA Modules:
  0.0 106.2 jit_solution(5171583547596327163)
XLA Ops:
  0.0 0.0 copy-start
  0.0 1.6 %copy-done = bf16[32,1,2,128,128]{4,3,2,1,0:T(8,128)(2,1)S(1)} copy-done((bf16[32,1,2,128,128]{4,3,2,1,0:T(8,128)(2,1)S(1)}, bf16[32,1,2,128,128]{4,3,2,1,0:T(8,128)(2,1)}, u32[]{:S(2)}) %copy-start) | copy-done | bytes 2097176
  1.6 0.0 copy-start.1
  1.6 0.9 copy-done.1
  2.5 0.0 copy-start.2
  2.5 0.9 copy-done.2
  3.5 0.0 copy-start.3
  3.5 0.9 copy-done.3
  4.4 0.0 copy-start.4
  4.4 0.9 copy-done.4
  5.3 0.0 copy-start.5
  5.3 0.8 copy-done.5
  6.0 0.0 copy-start.6
  6.0 0.8 copy-done.6
  6.8 0.0 copy-start.7
  6.8 0.7 copy-done.7
  7.5 98.1 %shard_map.82 = f32[512,128]{1,0:T(8,128)S(1)} custom-call(bf16[512,128]{1,0:T(8,128)(2,1)S(1)} %bitcast.11, bf16[512,128]{1,0:T(8,128)(2,1)S(1)} %bitcast.12, bf16[16,128]{1,0:T(8,128)(2,1)S(1)} %bitcast.15, bf16[128,128]{1,0:T(8,128)(2,1)S(1)} %bitcast.13, bf16[128,128]{1,0:T(8,128)(2,1)S(1)} %bitcast.14, bf16[32,2,128,128]{3,2,1,0:T(8,128)(2,1)S(1)} %bitcast.9, ...), custom_call_target="tpu_custom_call" | custom-call | tf_op jit(solution)/shard_map/pallas_call | solution.py:351
  105.5 0.7 copy.11
Async XLA Ops:
  0.0 1.6 %copy-start = (bf16[32,1,2,128,128]{4,3,2,1,0:T(8,128)(2,1)S(1)}, bf16[32,1,2,128,128]{4,3,2,1,0:T(8,128)(2,1)}, u32[]{:S(2)}) copy-start(bf16[32,1,2,128,128]{4,3,2,1,0:T(8,128)(2,1)} %param.13) | copy-start | bytes 6291460
  1.6 0.9 copy-start.1
  2.5 0.9 copy-start.2
  3.5 0.9 copy-start.3
  4.4 0.9 copy-start.4
  5.3 0.8 copy-start.5
  6.0 0.8 copy-start.6
  6.8 0.7 copy-start.7

commit v2 on v1

v2 whole, which is shorter than its diff:
```python
import functools
import math

import jax
import jax.numpy as jnp
import numpy as np
from jax import lax
from jax.experimental import pallas as pl
from jax.experimental.pallas import tpu as pltpu
from jax.sharding import PartitionSpec as P

MESH = pl.DeviceIdType.MESH
F32 = jnp.float32
CHUNKS = 4
LEAD = 4
BF16 = jnp.bfloat16


def split(value):
    high = value.astype(BF16)
    low = (value - high.astype(F32)).astype(BF16)
    return high, low


def dot(a, b):
    return jnp.dot(a, b, preferred_element_type=F32)


def tables(total, blocks):
    ids = np.arange(total)
    theta = 2.0 * math.pi / total * ((ids[:, None] * ids[None, :]) % total)
    gamma = 0.5 ** (ids / total)
    here = total // blocks

    def three(table):
        high = table.astype(np.float32).astype(jnp.bfloat16)
        low = (table - high.astype(np.float64)).astype(np.float32).astype(jnp.bfloat16)
        return np.concatenate([high, high, low], -1)

    half = here // 2
    cosine = (np.cos(theta) * gamma).reshape(blocks, 2, half, total)
    sine = (-np.sin(theta) * gamma).reshape(blocks, 2, half, total)
    forward = three(np.concatenate([cosine, sine], 2))
    back = 1.0 / (total * gamma[:, None])
    cosine = (np.cos(theta) * back).reshape(total, blocks, 2, half).transpose(1, 2, 0, 3)
    sine = (-np.sin(theta) * back).reshape(total, blocks, 2, half).transpose(1, 2, 0, 3)
    inverse = three(np.concatenate([cosine, sine], 3))
    return forward, inverse


def kernel(
    n_tm, n_sp, chunks, lead, cases, forcing_hbm, iterate_hbm, initial_hbm, stiff_hbm, coup_hbm,
    pivots_hbm, tf_hbm, ti_hbm, out,
    forcing, iterate, initial, stiff, coup, pivots, tf, ti,
    it_below, it_above, c_below, c_above, prior0, gath, weights, c2, ct2,
    spec, spec_out, pv, q_in, q_out, x_in, solved, other, contrib, rs1, rs2,
    ld, nb_send, nb_recv, p_send, p_recv, ag_send, ag_recv, s_send, s_recv,
    f_send, f_recv, b_send, b_recv, e_send, e_recv, r1_send, r1_recv, r2_send, r2_recv,
):
    tm, sp = lax.axis_index("tm"), lax.axis_index("span")
    rows, dof = iterate.shape
    steps = rows // cases
    total = steps * n_tm
    half = steps // 2
    per = half // chunks
    size = per * cases
    y = sp % 2
    peer = sp + 1 - 2 * y
    n_x = n_tm // 2
    core, x = tm % 2, tm // 2
    sib = 2 * x + 1 - core
    last = n_sp - 1
    has_below, has_above = sp > 0, sp < last
    pair_below, pair_above = sp > 1, sp < last - 1

    def copy(src, dst, send, recv, **where):
        return pltpu.make_async_remote_copy(
            src_ref=src, dst_ref=dst, send_sem=send, recv_sem=recv, device_id=where, device_id_type=MESH
        )

    loads = [
        pltpu.make_async_copy(src, dst, ld.at[i])
        for i, (src, dst) in enumerate(
            (
                (iterate_hbm, iterate),
                (stiff_hbm, stiff),
                (forcing_hbm, forcing),
                (initial_hbm, initial),
                (coup_hbm, coup),
                (tf_hbm.at[tm], tf),
                (ti_hbm.at[tm], ti),
                (pivots_hbm.at[pl.ds(y * half, half)], pivots.at[y]),
            )
        )
    ]
    for load in loads:
        load.start()

    def block(b):
        return pl.ds(pl.multiple_of(b * rows, rows), rows)

    barrier = pltpu.get_barrier_semaphore()
    for i in range(1, n_tm):
        pl.semaphore_signal(barrier, inc=1, device_id={"tm": (tm + i) % n_tm}, device_id_type=MESH)

    @pl.when(has_below)
    def _():
        pl.semaphore_signal(barrier, inc=1, device_id={"span": sp - 1}, device_id_type=MESH)

    @pl.when(has_above)
    def _():
        pl.semaphore_signal(barrier, inc=1, device_id={"span": sp + 1}, device_id_type=MESH)

    @pl.when(pair_below)
    def _():
        pl.semaphore_signal(barrier, inc=1, device_id={"span": sp - 2}, device_id_type=MESH)

    @pl.when(pair_above)
    def _():
        pl.semaphore_signal(barrier, inc=1, device_id={"span": sp + 2}, device_id_type=MESH)

    pl.semaphore_wait(
        barrier,
        n_tm - 1 + sum(t.astype(jnp.int32) for t in (has_below, has_above, pair_below, pair_above)),
    )

    to_up = copy(iterate_hbm, it_below, nb_send.at[0], nb_recv.at[0], span=sp + 1)
    to_down = copy(iterate_hbm, it_above, nb_send.at[1], nb_recv.at[1], span=sp - 1)
    c_up = copy(coup_hbm, c_below, nb_send.at[2], nb_recv.at[2], span=sp + 1)
    c_down = copy(coup_hbm, c_above, nb_send.at[4], nb_recv.at[4], span=sp - 1)
    to_next = copy(
        iterate_hbm.at[pl.ds(rows - cases, cases)], prior0, nb_send.at[3], nb_recv.at[3], tm=tm + 1
    )

    def p_copy(c):
        return copy(
            pivots_hbm.at[pl.ds((1 - y) * half + c * per, per)], pivots.at[y, pl.ds(c * per, per)],
            p_send.at[c], p_recv.at[c], span=peer,
        )

    @pl.when(tm < n_tm - 1)
    def _():
        to_next.start()

    @pl.when(has_above)
    def _():
        to_up.start()
        c_up.start()

    @pl.when(has_below)
    def _():
        to_down.start()

    @pl.when(y == 1)
    def _():
        c_down.start()

    for c in range(chunks):
        p_copy(c).start()

    mine = block(tm)
    for load in loads[:5]:
        load.wait()
    it_wide = iterate[...].astype(F32)
    own = forcing[...].astype(F32) - it_wide - dot(iterate[...], stiff[...])
    own = own + jnp.concatenate([jnp.zeros((cases, dof), F32), it_wide[: rows - cases]], 0)
    gath[mine] = own
    first = pl.ds(pl.multiple_of(tm * rows, rows), cases)

    def build(p, k):
        real, imag = pivots[p, k, 0], pivots[p, k, 1]
        weights[p, k, :dof, :dof] = real
        weights[p, k, dof:, dof:] = real
        weights[p, k, :dof, dof:] = imag
        weights[p, k, dof:, :dof] = -imag

    def build_own(k, carry):
        build(y, k)
        return carry

    @pl.when(tm == 0)
    def _():
        gath[first] = gath[first] + initial[...].astype(F32)

    @pl.when(tm > 0)
    def _():
        to_next.wait_recv()
        gath[first] = gath[first] + prior0[...].astype(F32)

    @pl.when(has_above)
    def _():
        to_down.wait_recv()
        gath[mine] = gath[mine] - lax.dot_general(
            it_above[...], coup[...], (((1,), (1,)), ((), ())), preferred_element_type=F32
        )

    @pl.when(has_below)
    def _():
        to_up.wait_recv()
        c_up.wait_recv()
        gath[mine] = gath[mine] - dot(it_below[...], c_below[...])

    def send_block(b, slot, peer):
        at = block(b)
        return copy(gath.at[at], gath.at[at], ag_send.at[slot], ag_recv.at[b], tm=peer)

    for i in range(1, n_x):
        send_block(tm, i, 2 * ((x + i) % n_x) + core).start()
    send_block(tm, 0, sib).start()

    @pl.when(y == 1)
    def _():
        c_down.wait_send()

    @pl.when(y == 0)
    def _():
        c_down.wait_recv()

    zero = jnp.zeros((dof, dof), BF16)
    bonds = (
        jnp.where(y == 0, coup[...], c_below[...]), jnp.where(y == 0, c_above[...], coup[...])
    )
    for p in range(2):
        for ref, value in ((c2, bonds[p]), (ct2, bonds[p].astype(F32).T.astype(BF16))):
            ref[p, :dof, :dof] = value
            ref[p, dof:, dof:] = value
            ref[p, :dof, dof:] = zero
            ref[p, dof:, :dof] = zero
    loads[7].wait()
    lax.fori_loop(0, half, build_own, 0)

    @pl.when(sp < 2)
    def _():
        q_in[...] = jnp.zeros_like(q_in)

    for load in loads[5:7]:
        load.wait()
    for i in range(1, n_x):
        b = 2 * ((x + n_x - i) % n_x) + core
        send_block(b, 0, sib).wait_recv()
        send_block(b, n_x + i, sib).start()
    for i in range(n_x):
        send_block(2 * ((x + n_x - i) % n_x) + 1 - core, 0, sib).wait_recv()

    def at_chunk(c):
        return pl.ds(pl.multiple_of(c * size, size), size)

    def s_copy(c):
        at = at_chunk(c)
        return copy(spec_out.at[:, at], spec.at[y, :, at], s_send.at[c], s_recv.at[c], span=peer)

    def transform(which, put):
        for case in range(0, cases, 2):
            value = jnp.concatenate(
                [gath[pl.ds(case + i, total, stride=cases), :] for i in range(2)], 1
            )
            high, low = split(value)
            result = dot(tf[which], jnp.concatenate([high, low, high], 0))
            for i in range(2):
                part = result[:, i * dof : (i + 1) * dof]
                put(0, pl.ds(case + i, half, stride=cases), part[:half])
                put(1, pl.ds(case + i, half, stride=cases), part[half:])

    def put_out(part, at, value):
        spec_out[part, at, :] = value

    def put_own(part, at, value):
        spec[y, part, at, :] = value

    transform(1 - y, put_out)
    for c in range(chunks):
        s_copy(c).start()
    transform(y, put_own)

    def f_copy(c):
        at = at_chunk(c)
        return copy(q_out.at[:, at], q_in.at[:, at], f_send.at[c], f_recv.at[c], span=sp + 2)

    def b_copy(c):
        at = at_chunk(c)
        return copy(solved.at[0, :, at], x_in.at[:, at], b_send.at[c], b_recv.at[c], span=sp - 2)

    def e_copy(c):
        at = at_chunk(c)
        return copy(
            solved.at[1 - y, :, at], other.at[:, at], e_send.at[c], e_recv.at[c], span=peer
        )

    def wide(ref, at):
        return jnp.concatenate([ref[0, at, :], ref[1, at, :]], 1)

    def put(ref, at, value):
        ref[0, at, :] = value[:, :dof]
        ref[1, at, :] = value[:, dof:]

    def times_pivots(value, p, c):
        high, low = split(value)
        parts = []
        for f in range(per):
            at = slice(f * cases, (f + 1) * cases)
            both = dot(jnp.concatenate([high[at], low[at]], 0), weights[p, c * per + f])
            parts.append(both[:cases] + both[cases:])
        return jnp.concatenate(parts, 0)

    def times_bond(value, bond):
        both = dot(jnp.concatenate(split(value), 0), bond)
        return both[:size] + both[size:]

    def finish(c, at, upper, lower):
        put(solved.at[1], at, upper)
        upper = lower - times_pivots(times_bond(upper, ct2[0]), 0, c)
        put(solved.at[0], at, upper)

        @pl.when(pair_below)
        def _():
            b_copy(c).start()

        e_copy(c).start()

    def up(c):
        at = at_chunk(c)
        p_copy(c).wait_recv()
        for f in range(per):
            build(1 - y, c * per + f)
        s_copy(c).wait_recv()

        @pl.when(pair_below)
        def _():
            f_copy(c).wait_recv()

        lower = times_pivots(wide(spec.at[0], at) - wide(q_in, at), 0, c)
        upper = times_pivots(wide(spec.at[1], at) - times_bond(lower, c2[0]), 1, c)

        @pl.when(pair_above)
        def _():
            put(q_out, at, times_bond(upper, c2[1]))
            f_copy(c).start()
            put(pv.at[0], at, lower)
            put(pv.at[1], at, upper)

        @pl.when(sp >= last - 1)
        def _():
            finish(c, at, upper, lower)

    def down(c):
        at = at_chunk(c)
        b_copy(c).wait_recv()
        upper = wide(pv.at[1], at) - times_pivots(times_bond(wide(x_in, at), ct2[1]), 1, c)
        finish(c, at, upper, wide(pv.at[0], at))

    lag = jnp.minimum(chunks, lead * ((last - sp) // 2))

    def turn(t, carry):
        @pl.when(t < chunks)
        def _():
            up(t)

        @pl.when(pair_above & (t >= lag) & (t < lag + chunks))
        def _():
            down(t - lag)

        return carry

    lax.fori_loop(0, 2 * chunks, turn, 0)
    for c in range(chunks):
        e_copy(c).wait_recv()

    def back(read, which, case):
        value = jnp.concatenate(
            [
                jnp.concatenate(
                    [read(p, pl.ds(case + i, half, stride=cases)) for p in range(2)], 0
                )
                for i in range(2)
            ],
            1,
        )
        high, low = split(value)
        return dot(ti[which], jnp.concatenate([high, low, high], 0))

    for case in range(0, cases, 2):
        result = back(lambda p, at: solved[y, p, at, :], y, case)
        result = result + back(lambda p, at: other[p, at, :], 1 - y, case)
        for i in range(2):
            contrib[pl.ds(case + i, total, stride=cases), :] = result[:, i * dof : (i + 1) * dof]

    def r1_copy(i):
        there = (x + i) % n_x
        return copy(
            contrib.at[block(2 * there + 1 - core)], rs1.at[i], r1_send.at[i], r1_recv.at[i], tm=sib
        )

    def r2_copy(i):
        there = (x + i) % n_x
        return copy(
            contrib.at[block(2 * there + core)], rs2.at[i], r2_send.at[i], r2_recv.at[i],
            tm=2 * there + core,
        )

    order = list(range(1, n_x)) + [0]
    for i in order:
        r1_copy(i).start()
    for i in order:
        r1_copy(i).wait_recv()
        at = block(2 * ((x + i) % n_x) + core)
        contrib[at] = contrib[at] + rs1[i]
        if i:
            r2_copy(i).start()
    result = contrib[mine] + iterate[...].astype(F32)
    for i in range(1, n_x):
        r2_copy(i).wait_recv()
        result = result + rs2[i]
    out[...] = result

    @pl.when(tm < n_tm - 1)
    def _():
        to_next.wait_send()

    @pl.when(has_above)
    def _():
        to_up.wait_send()
        c_up.wait_send()

    @pl.when(has_below)
    def _():
        to_down.wait_send()

    for slot in range(2 * n_x):
        if slot != n_x:
            send_block(tm, slot, sib).wait_send()

    for c in range(chunks):
        p_copy(c).wait_send()
        s_copy(c).wait_send()
        e_copy(c).wait_send()

    @pl.when(pair_above)
    def _():
        for c in range(chunks):
            f_copy(c).wait_send()

    @pl.when(pair_below)
    def _():
        for c in range(chunks):
            b_copy(c).wait_send()

    for i in range(n_x):
        r1_copy(i).wait_send()
    for i in range(1, n_x):
        r2_copy(i).wait_send()


def on_device(n_tm, n_sp, forcing, iterate, initial, stiffness, coupling, pivots):
    steps, planes, cases, dof = forcing.shape
    assert planes == 1 and n_tm % 2 == 0 and n_sp % 2 == 0 and steps % 2 == 0
    rows, total, n_x, half = steps * cases, steps * n_tm, n_tm // 2, steps // 2
    chunks = math.gcd(half, CHUNKS)
    forward, inverse = tables(total, n_tm)
    state = pltpu.VMEM((2, half * cases, dof), F32)
    both = pltpu.VMEM((2, 2, half * cases, dof), F32)
    dma = pltpu.SemaphoreType.DMA
    result = pl.pallas_call(
        functools.partial(kernel, n_tm, n_sp, chunks, LEAD, cases),
        out_shape=jax.ShapeDtypeStruct((rows, dof), F32),
        in_specs=[pl.BlockSpec(memory_space=pl.ANY)] * 8,
        out_specs=pl.BlockSpec(memory_space=pltpu.VMEM),
        scratch_shapes=[
            pltpu.VMEM((rows, dof), BF16),
            pltpu.VMEM((rows, dof), BF16),
            pltpu.VMEM((cases, dof), BF16),
            pltpu.VMEM((dof, dof), BF16),
            pltpu.VMEM((dof, dof), BF16),
            pltpu.VMEM((2, half, 2, dof, dof), BF16),
            pltpu.VMEM(forward.shape[1:], BF16),
            pltpu.VMEM(inverse.shape[1:], BF16),
            pltpu.VMEM((rows, dof), BF16),
            pltpu.VMEM((rows, dof), BF16),
            pltpu.VMEM((dof, dof), BF16),
            pltpu.VMEM((dof, dof), BF16),
            pltpu.VMEM((cases, dof), BF16),
            pltpu.VMEM((total * cases, dof), F32),
            pltpu.VMEM((2, half, 2 * dof, 2 * dof), BF16),
            pltpu.VMEM((2, 2 * dof, 2 * dof), BF16),
            pltpu.VMEM((2, 2 * dof, 2 * dof), BF16),
            both, state, both, state, state, state, both, state,
            pltpu.VMEM((total * cases, dof), F32),
            pltpu.VMEM((n_x, rows, dof), F32),
            pltpu.VMEM((n_x, rows, dof), F32),
            dma((8,)), dma((5,)), dma((5,)), dma((chunks,)), dma((chunks,)),
            dma((2 * n_x,)), dma((n_tm,)),
        ]
        + [dma((chunks,))] * 8
        + [dma((n_x,))] * 4,
        compiler_params=pltpu.CompilerParams(
            collective_id=0, has_side_effects=True, vmem_limit_bytes=60 * 2**20
        ),
    )(
        forcing.reshape(rows, dof),
        iterate.reshape(rows, dof),
        initial.reshape(cases, dof),
        stiffness.reshape(dof, dof),
        coupling.reshape(dof, dof),
        pivots.reshape(steps, 2, dof, dof),
        jnp.asarray(forward),
        jnp.asarray(inverse),
    )
    return result.reshape(steps, 1, cases, dof)


def solution(mesh):
    return jax.shard_map(
        functools.partial(on_device, mesh.shape["tm"], mesh.shape["span"]),
        mesh=mesh,
        in_specs=(
            P("tm", "span", None, None),
            P("tm", "span", None, None),
            P("span", None, None),
            P("span", None, None),
            P("span", None, None),
            P("tm", "span", None, None, None),
        ),
        out_specs=P("tm", "span", None, None),
        check_vma=False,
    )
```

time: 107 us -> 79.5 us (0.74)
  Pallas kernels: 98.1 us -> 77.7 us
  local copies, waits for them, and re-layouts: 8.18 us -> 1.67 us
    pallas_call x1, Pallas kernels: 98.1 us -> 77.7 us  [on_device(): pl.pallas_call(functools.partial(kernel, n_tm, n_sp, chunks, LEAD, cases)...]
    unnamed x17 -> x1, local copies, waits for them, and re-layouts: 8.18 us -> 1.67 us
where the time goes in v2:
time: 79.5 us; the launch traced here: 79.4 us
  Pallas kernels  77.7 us (98%)
  local copies, waits for them, and re-layouts  1.67 us (2%)
    pallas_call x1, Pallas kernels, on_device(): pl.pallas_call(functools.partial(kernel, n_tm, n_sp, chunks, LEAD, cases)...  77.7 us
    unnamed x1, local copies, waits for them, and re-layouts  1.67 us

profile of v2, /device:TPU:1, one launch (start us, length us, event | category | flops | bytes accessed | tf_op | source)
XLA Modules:
  0.0 79.4 jit_solution(15277284133630053307)
XLA Ops:
  0.0 77.7 %shard_map.82 = f32[512,128]{1,0:T(8,128)} custom-call(bf16[512,128]{1,0:T(8,128)(2,1)} %bitcast.11, bf16[512,128]{1,0:T(8,128)(2,1)} %bitcast.12, bf16[16,128]{1,0:T(8,128)(2,1)} %bitcast.15, bf16[128,128]{1,0:T(8,128)(2,1)} %bitcast.13, bf16[128,128]{1,0:T(8,128)(2,1)} %bitcast.14, bf16[32,2,128,128]{3,2,1,0:T(8,128)(2,1)} %bitcast.9, ...), custom_call_target="tpu_custom_call" | custom-call | tf_op jit(solution)/shard_map/pallas_call | solution.py:462
  77.7 1.7 %copy.11 = f32[32,1,16,128]{3,2,1,0:T(8,128)} copy(f32[32,1,16,128]{3,2,1,0:T(8,128)} %bitcast.10) | data formatting | bytes 524288

commit v3 on v2

--- a/solution.py
+++ b/solution.py
@@ -11,8 +11,9 @@
 
 MESH = pl.DeviceIdType.MESH
 F32 = jnp.float32
-CHUNKS = 4
-LEAD = 4
+CHUNKS = 8
+LEAD = 8
+EARLY = 5
 BF16 = jnp.bfloat16
 
 
@@ -128,6 +129,9 @@
     to_down = copy(iterate_hbm, it_above, nb_send.at[1], nb_recv.at[1], span=sp - 1)
     c_up = copy(coup_hbm, c_below, nb_send.at[2], nb_recv.at[2], span=sp + 1)
     c_down = copy(coup_hbm, c_above, nb_send.at[4], nb_recv.at[4], span=sp - 1)
+    on_up = copy(it_above, it_below, nb_send.at[5], nb_recv.at[5], span=sp + 2)
+    on_down = copy(it_below, it_above, nb_send.at[6], nb_recv.at[6], span=sp - 2)
+    c_on = copy(c_above, c_below, nb_send.at[7], nb_recv.at[7], span=sp + 2)
     to_next = copy(
         iterate_hbm.at[pl.ds(rows - cases, cases)], prior0, nb_send.at[3], nb_recv.at[3], tm=tm + 1
     )
@@ -142,20 +146,18 @@
     def _():
         to_next.start()
 
-    @pl.when(has_above)
+    @pl.when(y == 0)
     def _():
         to_up.start()
         c_up.start()
 
-    @pl.when(has_below)
+    @pl.when(y == 1)
     def _():
         to_down.start()
-
-    @pl.when(y == 1)
-    def _():
         c_down.start()
 
-    for c in range(chunks):
+    early = min(EARLY, chunks)
+    for c in range(early):
         p_copy(c).start()
 
     mine = block(tm)
@@ -187,18 +189,51 @@
         to_next.wait_recv()
         gath[first] = gath[first] + prior0[...].astype(F32)
 
-    @pl.when(has_above)
+    @pl.when(y == 0)
     def _():
         to_down.wait_recv()
+        c_down.wait_recv()
+
+        @pl.when(pair_above)
+        def _():
+            on_up.start()
+            c_on.start()
+
+    @pl.when(y == 1)
+    def _():
+        to_up.wait_recv()
+        c_up.wait_recv()
+
+        @pl.when(pair_below)
+        def _():
+            on_down.start()
+
+    def from_above():
         gath[mine] = gath[mine] - lax.dot_general(
             it_above[...], coup[...], (((1,), (1,)), ((), ())), preferred_element_type=F32
         )
 
-    @pl.when(has_below)
-    def _():
-        to_up.wait_recv()
-        c_up.wait_recv()
+    def from_below():
         gath[mine] = gath[mine] - dot(it_below[...], c_below[...])
+
+    @pl.when(y == 0)
+    def _():
+        from_above()
+
+        @pl.when(pair_below)
+        def _():
+            on_up.wait_recv()
+            c_on.wait_recv()
+            from_below()
+
+    @pl.when(y == 1)
+    def _():
+        from_below()
+
+        @pl.when(pair_above)
+        def _():
+            on_down.wait_recv()
+            from_above()
 
     def send_block(b, slot, peer):
         at = block(b)
@@ -207,14 +242,6 @@
     for i in range(1, n_x):
         send_block(tm, i, 2 * ((x + i) % n_x) + core).start()
     send_block(tm, 0, sib).start()
-
-    @pl.when(y == 1)
-    def _():
-        c_down.wait_send()
-
-    @pl.when(y == 0)
-    def _():
-        c_down.wait_recv()
 
     zero = jnp.zeros((dof, dof), BF16)
     bonds = (
@@ -270,6 +297,8 @@
     transform(1 - y, put_out)
     for c in range(chunks):
         s_copy(c).start()
+    for c in range(early, chunks):
+        p_copy(c).start()
     transform(y, put_own)
 
     def f_copy(c):
@@ -416,14 +445,24 @@
     def _():
         to_next.wait_send()
 
-    @pl.when(has_above)
+    @pl.when(y == 0)
     def _():
         to_up.wait_send()
         c_up.wait_send()
 
-    @pl.when(has_below)
+        @pl.when(pair_above)
+        def _():
+            on_up.wait_send()
+            c_on.wait_send()
+
+    @pl.when(y == 1)
     def _():
         to_down.wait_send()
+        c_down.wait_send()
+
+        @pl.when(pair_below)
+        def _():
+            on_down.wait_send()
 
     for slot in range(2 * n_x):
         if slot != n_x:
@@ -486,7 +525,7 @@
             pltpu.VMEM((total * cases, dof), F32),
             pltpu.VMEM((n_x, rows, dof), F32),
             pltpu.VMEM((n_x, rows, dof), F32),
-            dma((8,)), dma((5,)), dma((5,)), dma((chunks,)), dma((chunks,)),
+            dma((8,)), dma((8,)), dma((8,)), dma((chunks,)), dma((chunks,)),
             dma((2 * n_x,)), dma((n_tm,)),
         ]
         + [dma((chunks,))] * 8

time: 79.5 us -> 73.1 us (0.919)
  Pallas kernels: 77.7 us -> 71.2 us
    pallas_call x1, Pallas kernels: 77.7 us -> 71.2 us  [on_device(): pl.pallas_call(functools.partial(kernel, n_tm, n_sp, chunks, LEAD, cases)...]
where the time goes in v3:
time: 73.1 us; the launch traced here: 72.9 us
  Pallas kernels  71.2 us (97%)
  local copies, waits for them, and re-layouts  1.67 us (2%)
    pallas_call x1, Pallas kernels, on_device(): pl.pallas_call(functools.partial(kernel, n_tm, n_sp, chunks, LEAD, cases)...  71.2 us
    unnamed x1, local copies, waits for them, and re-layouts  1.67 us

profile of v3, /device:TPU:1, one launch (start us, length us, event | category | flops | bytes accessed | tf_op | source)
XLA Modules:
  0.0 72.9 jit_solution(13829262167164126590)
XLA Ops:
  0.0 71.2 %shard_map.82 = f32[512,128]{1,0:T(8,128)} custom-call(bf16[512,128]{1,0:T(8,128)(2,1)} %bitcast.11, bf16[512,128]{1,0:T(8,128)(2,1)} %bitcast.12, bf16[16,128]{1,0:T(8,128)(2,1)} %bitcast.15, bf16[128,128]{1,0:T(8,128)(2,1)} %bitcast.13, bf16[128,128]{1,0:T(8,128)(2,1)} %bitcast.14, bf16[32,2,128,128]{3,2,1,0:T(8,128)(2,1)} %bitcast.9, ...), custom_call_target="tpu_custom_call" | custom-call | tf_op jit(solution)/shard_map/pallas_call | solution.py:501
  71.2 1.7 %copy.11 = f32[32,1,16,128]{3,2,1,0:T(8,128)} copy(f32[32,1,16,128]{3,2,1,0:T(8,128)} %bitcast.10) | data formatting | bytes 524288

commit v4 on v3

--- a/solution.py
+++ b/solution.py
@@ -391,9 +391,6 @@
         return carry
 
     lax.fori_loop(0, 2 * chunks, turn, 0)
-    for c in range(chunks):
-        e_copy(c).wait_recv()
-
     def back(read, which, case):
         value = jnp.concatenate(
             [
@@ -409,9 +406,15 @@
 
     for case in range(0, cases, 2):
         result = back(lambda p, at: solved[y, p, at, :], y, case)
-        result = result + back(lambda p, at: other[p, at, :], 1 - y, case)
         for i in range(2):
             contrib[pl.ds(case + i, total, stride=cases), :] = result[:, i * dof : (i + 1) * dof]
+    for c in range(chunks):
+        e_copy(c).wait_recv()
+    for case in range(0, cases, 2):
+        result = back(lambda p, at: other[p, at, :], 1 - y, case)
+        for i in range(2):
+            at = pl.ds(case + i, total, stride=cases)
+            contrib[at, :] = contrib[at, :] + result[:, i * dof : (i + 1) * dof]
 
     def r1_copy(i):
         there = (x + i) % n_x

time: 73.1 us -> 73.2 us (level)
  no operation moved by 1% of the time
where the time goes in v4:
time: 73.2 us; the launch traced here: 73.1 us
  Pallas kernels  71.4 us (98%)
  local copies, waits for them, and re-layouts  1.67 us (2%)
    pallas_call x1, Pallas kernels, on_device(): pl.pallas_call(functools.partial(kernel, n_tm, n_sp, chunks, LEAD, cases)...  71.4 us
    unnamed x1, local copies, waits for them, and re-layouts  1.67 us

profile of v4, /device:TPU:1, one launch (start us, length us, event | category | flops | bytes accessed | tf_op | source)
XLA Modules:
  0.0 73.1 jit_solution(4847239467542114190)
XLA Ops:
  0.0 71.4 %shard_map.82 = f32[512,128]{1,0:T(8,128)} custom-call(bf16[512,128]{1,0:T(8,128)(2,1)} %bitcast.11, bf16[512,128]{1,0:T(8,128)(2,1)} %bitcast.12, bf16[16,128]{1,0:T(8,128)(2,1)} %bitcast.15, bf16[128,128]{1,0:T(8,128)(2,1)} %bitcast.13, bf16[128,128]{1,0:T(8,128)(2,1)} %bitcast.14, bf16[32,2,128,128]{3,2,1,0:T(8,128)(2,1)} %bitcast.9, ...), custom_call_target="tpu_custom_call" | custom-call | tf_op jit(solution)/shard_map/pallas_call | solution.py:504
  71.4 1.7 %copy.11 = f32[32,1,16,128]{3,2,1,0:T(8,128)} copy(f32[32,1,16,128]{3,2,1,0:T(8,128)} %bitcast.10) | data formatting | bytes 524288
